TPU v7x, 512 devices: a whole 4x4x16 slice. The times are simulated.
512 devices in a mesh: seq: 64 (over z, y), tp: 8 (over x, core).
Axes of the slice: x: 4, y: 4, z: 16, core: 2. Of those that a mesh axis runs over, the one named last changes fastest.
Arguments:
- query_proj: bfloat16 [4096, 8192], P('tp', 'seq'), may hold values from -6 to 6
- key_proj: bfloat16 [4096, 8192], P('tp', 'seq'), may hold values from -6 to 6
- value_proj: bfloat16 [4096, 8192], P('tp', 'seq'), may hold values from -6 to 6
- short_taps: float32 [3, 3, 4096], P(None, None, 'tp'), may hold values from -3.5 to 3.5
- long_filters: float32 [4096, 8192], P(('tp', 'seq')), may hold values from -2 to 2
- out_weight: bfloat16 [4096, 8192], P('seq', 'tp'), may hold values from -0.09375 to 0.09375
Outputs:
- block_out: bfloat16 [8192, 8192], P('seq', 'tp')
All inputs are finite; a program needn't handle non-finite values.
Results may differ from a plain program's by a relative error of at most 0.0058.
Values may be sent and summed in bfloat16 or wider, within the bound.
A program may use at most 64 MiB of HBM per device.

v0:
```python
import math

import jax
import jax.numpy as jnp
from jax import lax
from jax.sharding import PartitionSpec as P

precise = lax.Precision.HIGHEST


def shifted(value, axis, steps):
    count = lax.axis_size(axis)
    initial, last = (max(0, -steps), min(count, count - steps))
    return lax.ppermute(value, axis, [(source, source + steps) for source in range(initial, last)])


def short_filter(extended, tap_weights):
    return (
        tap_weights[0][:, None] * extended[:, 2:]
        + tap_weights[1][:, None] * extended[:, 1:-1]
        + tap_weights[2][:, None] * extended[:, :-2]
    )


def phase_table(period, out_size, in_size, direction):
    out_index = lax.broadcasted_iota(jnp.int32, (out_size, in_size), 0)
    in_index = lax.broadcasted_iota(jnp.int32, (out_size, in_size), 1)
    phase_angle = (out_index * in_index % period).astype(jnp.float32) * (
        direction * 2.0 * math.pi / period
    )
    return (jnp.cos(phase_angle), jnp.sin(phase_angle))


def left_apply(phase, signal):
    return jnp.einsum("kn,cnm->ckm", phase, signal, precision=precise)


def right_apply(signal, phase):
    return jnp.einsum("ckn,nm->ckm", signal, phase, precision=precise)


def forward_spectrum(signal, inner_size):
    channels_here, length = signal.shape
    period = 2 * length
    outer_size = period // inner_size
    blocks = signal.reshape(channels_here, outer_size // 2, inner_size)
    left_re, left_im = phase_table(outer_size, outer_size, outer_size // 2, -1.0)
    section_re = left_apply(left_re, blocks)
    section_im = left_apply(left_im, blocks)
    twist_re, twist_im = phase_table(period, outer_size, inner_size, -1.0)
    turned_re = section_re * twist_re - section_im * twist_im
    turned_im = section_re * twist_im + section_im * twist_re
    right_re, right_im = phase_table(inner_size, inner_size, inner_size, -1.0)
    spec_re = right_apply(turned_re, right_re) - right_apply(turned_im, right_im)
    spec_im = right_apply(turned_re, right_im) + right_apply(turned_im, right_re)
    return (spec_re, spec_im)


def inverse_signal(spec_re, spec_im, length, inner_size):
    channels_here = spec_re.shape[0]
    period = 2 * length
    outer_size = period // inner_size
    right_re, right_im = phase_table(inner_size, inner_size, inner_size, 1.0)
    mid_re = right_apply(spec_re, right_re) - right_apply(spec_im, right_im)
    mid_im = right_apply(spec_re, right_im) + right_apply(spec_im, right_re)
    twist_re, twist_im = phase_table(period, outer_size, inner_size, 1.0)
    turned_re = mid_re * twist_re - mid_im * twist_im
    turned_im = mid_re * twist_im + mid_im * twist_re
    left_re, left_im = phase_table(outer_size, outer_size // 2, outer_size, 1.0)
    signal = left_apply(left_re, turned_re) - left_apply(left_im, turned_im)
    return signal.reshape(channels_here, length) / period


def long_convolve(signal, filters, inner_size):
    length = signal.shape[1]
    data_re, data_im = forward_spectrum(signal, inner_size)
    filt_re, filt_im = forward_spectrum(filters, inner_size)
    prod_re = data_re * filt_re - data_im * filt_im
    prod_im = data_re * filt_im + data_im * filt_re
    return inverse_signal(prod_re, prod_im, length, inner_size)


def shards(query_proj, key_proj, value_proj, short_taps, long_filters, out_weight):
    tok_rows = query_proj.shape[1]
    inner_size = tok_rows // 2
    tail_cols = jnp.stack([query_proj[:, -2:], key_proj[:, -2:], value_proj[:, -2:]])
    before = shifted(tail_cols, "seq", 1)
    shorts = []
    for stream_index, stream in enumerate((query_proj, key_proj, value_proj)):
        extended = jnp.concatenate([before[stream_index], stream], axis=1).astype(jnp.float32)
        shorts.append(short_filter(extended, short_taps[stream_index]))
    query_short, key_short, value_short = shorts
    product = (key_short * value_short).astype(jnp.bfloat16)
    spread = lax.all_to_all(product, "seq", split_axis=0, concat_axis=1, tiled=True)
    mixed_conv = long_convolve(spread.astype(jnp.float32), long_filters, inner_size)
    returned = lax.all_to_all(mixed_conv, "seq", split_axis=1, concat_axis=0, tiled=True)
    gated_out = (query_short * returned).astype(jnp.bfloat16)
    full_rows = lax.all_gather(gated_out, "tp", axis=0, tiled=True)
    result = lax.dot_general(
        full_rows,
        lax.all_gather(out_weight, "seq", axis=0, tiled=True),
        (((0,), (0,)), ((), ())),
        preferred_element_type=jnp.float32,
    )
    return result.astype(jnp.bfloat16)


def solution(mesh):
    return jax.shard_map(
        shards,
        mesh=mesh,
        in_specs=(
            P("tp", "seq"),
            P("tp", "seq"),
            P("tp", "seq"),
            P(None, None, "tp"),
            P(("tp", "seq"), None),
            P("seq", "tp"),
        ),
        out_specs=P("seq", "tp"),
        check_vma=False,
    )
```

profile of v0, /device:TPU:6, one launch (start us, length us, event | category | flops | bytes accessed | tf_op | source)
XLA Modules:
  0.0 292.8 jit_solution(1270531788461723805)
XLA Ops:
  6.5 1.0 slice.94
  7.7 1.0 slice.95
  8.8 1.0 slice.96
  10.3 3.5 %collective-permute-start = (bf16[3,512,2]{2,1,0:T(8,128)(2,1)S(1)}, bf16[3,512,2]{2,1,0:T(8,128)(2,1)S(1)}, u32[]{:S(2)}, u32[]{:S(2)}) collective-permute-start(bf16[3,512,2]{2,1,0:T(8,128)(2,1)S(1)} %copy.25), channel_id=1, source_target_pairs={{0,8},{8,16},{16,24},{24,32},{32,40},{40,48},{48,56},{56,64},{64,7... | collective-permute-start | bytes 18440 | tf_op jit(solution)/shard_map/ppermute | solution.py:14
  14.1 1.1 reshape.82
  15.4 1.1 fusion.58
  16.5 1.1 fusion.61
  17.6 0.9 fusion.180
  18.4 0.8 fusion.4
  19.2 0.8 convolution_add_fusion.1
  20.3 1.8 collective-permute-done
  22.4 1.4 fusion.47
  23.8 20.5 %all-to-all-start = ((bf16[64,8,128]{2,1,0:T(8,128)(2,1)}), bf16[64,8,128]{2,1,0:T(8,128)(2,1)S(1)}, u32[]{:S(2)}, u32[]{:S(2)}) async-start(bf16[64,8,128]{2,1,0:T(8,128)(2,1)} %fusion.47), calls=%async_computation | async-start | bytes 262144 | tf_op jit(solution)/shard_map/all_to_all | solution.py:94
  44.3 0.8 fusion.6
  45.1 0.8 convolution_subtract_fusion.1
  45.9 15.1 %all-to-all-done = bf16[64,8,128]{2,1,0:T(8,128)(2,1)S(1)} async-done(((bf16[64,8,128]{2,1,0:T(8,128)(2,1)}), bf16[64,8,128]{2,1,0:T(8,128)(2,1)S(1)}, u32[]{:S(2)}, u32[]{:S(2)}) %all-to-all-start) | async-done | bytes 131104 | tf_op jit(solution)/shard_map/all_to_all | solution.py:94
  61.1 0.9 convolution_bitcast_fusion
  62.0 0.9 convolution_bitcast_fusion.1
  62.9 0.8 fusion.48
  63.7 0.8 fusion.49
  64.5 0.8 convolution_subtract_fusion.2
  65.3 0.9 multiply_add_fusion
  67.0 0.7 fusion.67
  69.2 1.1 fusion.11
  70.3 1.1 fusion.1
  71.7 1.1 copy.32
  72.8 4.6 %all-to-all-start.1 = ((f32[8,64,128]{2,0,1:T(8,128)}), f32[8,64,128]{2,0,1:T(8,128)S(1)}, u32[]{:S(2)}, u32[]{:S(2)}) async-start(f32[8,64,128]{2,0,1:T(8,128)} %copy.32), calls=%async_computation.1 | async-start | bytes 524288 | tf_op jit(solution)/shard_map/all_to_all | solution.py:96
  77.6 21.1 %all-to-all-done.1 = f32[8,64,128]{2,0,1:T(8,128)S(1)} async-done(((f32[8,64,128]{2,0,1:T(8,128)}), f32[8,64,128]{2,0,1:T(8,128)S(1)}, u32[]{:S(2)}, u32[]{:S(2)}) %all-to-all-start.1) | async-done | bytes 262176 | tf_op jit(solution)/shard_map/all_to_all | solution.py:96
  98.8 1.1 fusion.23
  100.6 19.3 %all-gather.3.cloned.1.call-done = bf16[4096,128]{1,0:T(8,128)(2,1)} async-done(((bf16[512,128]{1,0:T(8,128)(2,1)}), bf16[4096,128]{1,0:T(8,128)(2,1)}) %all-gather.3.cloned.1.call-update) | async-done | bytes 1048592 | tf_op jit(solution)/shard_map/all_gather | solution.py:98
  119.9 160.3 %all-gather.5.cloned.1.call-done = bf16[4096,1024]{1,0:T(8,128)(2,1)} async-done(((bf16[64,1024]{1,0:T(8,128)(2,1)}), bf16[4096,1024]{1,0:T(8,128)(2,1)}) %all-gather.5.cloned.1.call-update) | async-done | bytes 8388624 | tf_op jit(solution)/shard_map/all_gather | solution.py:101
  280.2 5.7 %convolution_convert_fusion = bf16[128,1024]{1,0:T(8,128)(2,1)} fusion(bf16[4096,128]{1,0:T(8,128)(2,1)} %all-gather.3.cloned.1.call-done, bf16[4096,1024]{1,0:T(8,128)(2,1)} %all-gather.5.cloned.1.call-done), kind=kOutput, calls=%fused_computation.8 | convolution fusion | flops 1073872896 | bytes 9699328 | tf_op jit(solution)/shard_map/dot_general | solution.py:99
  (28 shorter events, 5.2 us)
Async XLA Ops:
  6.5 15.6 %copy-start.1 = (bf16[512,128]{1,0:T(8,128)(2,1)S(1)}, bf16[512,128]{1,0:T(8,128)(2,1)}, u32[]{:S(2)}) copy-start(bf16[512,128]{1,0:T(8,128)(2,1)} %param.7) | copy-start | bytes 393220
  6.5 15.6 %copy-start = (bf16[512,128]{1,0:T(8,128)(2,1)S(1)}, bf16[512,128]{1,0:T(8,128)(2,1)}, u32[]{:S(2)}) copy-start(bf16[512,128]{1,0:T(8,128)(2,1)} %param.8) | copy-start | bytes 393220
  10.3 11.8 %collective-permute-start = (bf16[3,512,2]{2,1,0:T(8,128)(2,1)S(1)}, bf16[3,512,2]{2,1,0:T(8,128)(2,1)S(1)}, u32[]{:S(2)}, u32[]{:S(2)}) collective-permute-start(bf16[3,512,2]{2,1,0:T(8,128)(2,1)S(1)} %copy.25), channel_id=1, source_target_pairs={{0,8},{8,16},{16,24},{24,32},{32,40},{40,48},{48,56},{56,64},{64,7... | collective-permute-start | bytes 18440 | tf_op jit(solution)/shard_map/ppermute | solution.py:14
  23.8 37.2 %all-to-all-start = ((bf16[64,8,128]{2,1,0:T(8,128)(2,1)}), bf16[64,8,128]{2,1,0:T(8,128)(2,1)S(1)}, u32[]{:S(2)}, u32[]{:S(2)}) async-start(bf16[64,8,128]{2,1,0:T(8,128)(2,1)} %fusion.47), calls=%async_computation | async-start | bytes 262144 | tf_op jit(solution)/shard_map/all_to_all | solution.py:94
  64.5 13.0 %copy-start.2 = (bf16[512,128]{1,0:T(8,128)(2,1)S(1)}, bf16[512,128]{1,0:T(8,128)(2,1)}, u32[]{:S(2)}) copy-start(bf16[512,128]{1,0:T(8,128)(2,1)} %param.6) | copy-start | bytes 393220
  72.8 25.9 %all-to-all-start.1 = ((f32[8,64,128]{2,0,1:T(8,128)}), f32[8,64,128]{2,0,1:T(8,128)S(1)}, u32[]{:S(2)}, u32[]{:S(2)}) async-start(f32[8,64,128]{2,0,1:T(8,128)} %copy.32), calls=%async_computation.1 | async-start | bytes 524288 | tf_op jit(solution)/shard_map/all_to_all | solution.py:96
  77.4 42.5 %all-gather.3.cloned.1.call-start = ((), (), s32[]{:S(2)}) async-start(), calls=%async_computation.2 | async-start | bytes 1179648 | tf_op jit(solution)/shard_map/all_gather | solution.py:98
  99.8 180.4 %all-gather.5.cloned.1.call-start = ((), (), s32[]{:S(2)}) async-start(), calls=%async_computation.3 | async-start | bytes 8519680 | tf_op jit(solution)/shard_map/all_gather | solution.py:101
Sparse Core Ops, SparseCore 0:
  100.0 19.9 all-gather.2
  122.8 157.3 all-gather.4
where the time goes:
time: 293 us
  waiting for transfers between devices  218 us (74%)
  starting transfers between devices  28.7 us (10%)
  matrix products  21.1 us (7%)
  between operations  13.7 us (5%)
  local copies, waits for them, and re-layouts  7.47 us (3%)
  other arithmetic  3.41 us (1%)
    all_gather x1, waiting for transfers between devices, shards(): lax.all_gather(out_weight, 'seq', axis=0, tiled=True)  160 us
    all_to_all x1, waiting for transfers between devices, shards(): lax.all_to_all(mixed_conv, 'seq', split_axis=1, concat_axis=0, tiled=True)  21.1 us
    all_to_all x1, starting transfers between devices, shards(): lax.all_to_all(product, 'seq', split_axis=0, concat_axis=1, tiled=True)  20.5 us
    all_gather x1, waiting for transfers between devices, shards(): full_rows = lax.all_gather(gated_out, 'tp', axis=0, tiled=True)  19.3 us
    all_to_all x1, waiting for transfers between devices, shards(): lax.all_to_all(product, 'seq', split_axis=0, concat_axis=1, tiled=True)  15.1 us
    dot_general x12, matrix products, right_apply(): return jnp.einsum('ckn,nm->ckm', signal, phase, precision=precise)  9.29 us
  transfers between devices with their start and end apart: 5, of which 5 were waited for; matrix products, arithmetic and copies ran while one was open for 3% of the time, Pallas kernels for 0%

commit v1 on v0

v1 whole, which is shorter than its diff:
```python
import functools
import math

import jax
import jax.numpy as jnp
import numpy as np
from jax import lax
from jax.experimental import pallas as pl
from jax.experimental.pallas import tpu as pltpu
from jax.sharding import PartitionSpec as P

MESH = pl.DeviceIdType.MESH
F32 = jnp.float32
BF16 = jnp.bfloat16
BLOCK = 128
OWN = 8
exact = functools.partial(jnp.dot, precision=lax.Precision.HIGHEST, preferred_element_type=F32)


def tables(blocks):
    period = 2 * blocks * BLOCK
    padded = -(-(blocks + 1) // 8) * 8
    kb = np.arange(padded)[:, None]
    live = kb <= blocks
    left = 2 * math.pi * (kb * np.arange(blocks)[None, :] % (2 * blocks)) / (2 * blocks)
    forward = np.concatenate([live * np.cos(left), -(live * np.sin(left))], axis=0)
    share = np.where((kb == 0) | (kb == blocks), 1.0, 2.0) * live / period
    inverse = np.concatenate([share * np.cos(left), -(share * np.sin(left))], axis=0).T
    twist = 2 * math.pi * (kb * np.arange(BLOCK)[None, :] % period) / period
    turn = np.stack([np.cos(twist), -np.sin(twist)])
    right = np.arange(BLOCK)
    right = 2 * math.pi * (right[:, None] * right[None, :] % BLOCK) / BLOCK
    c, s = np.cos(right), np.sin(right)
    rows = np.block([[c, -s], [s, c]])
    return [np.asarray(a, np.float32) for a in (forward, inverse, turn, rows, np.ascontiguousarray(rows.T))]


def kernel(
    nz, ny, nx,
    q_ref, k_ref, v_ref, taps_ref, h_ref, w_ref,
    fwd_ref, inv_ref, turn_ref, rf_ref, ri_ref,
    out_ref,
    wide, edge_s, edge_r, prod, qout, yr, qr, zs, xin, rows, spec, ms, ar, gt, ga, wg, ps, pr, total,
    edge_sem, y_sem, z_send, z_recv, c_send, c_recv, x_send, x_recv, b_send, b_recv,
    w_send, w_recv, r_send, r_recv, own_sem,
):
    nc = 2
    nb = nz * ny
    ntp = nx * nc
    group = OWN * ntp
    seq = lax.axis_index("seq")
    tp = lax.axis_index("tp")
    z, y = seq // ny, seq % ny
    x, core = tp // nc, tp % nc

    def at(zz, yy):
        return (zz * ny + yy, tp)

    barrier = pltpu.get_barrier_semaphore()

    @pl.loop(1, nb)
    def _(d):
        pl.semaphore_signal(barrier, inc=1, device_id=((seq + d) % nb, tp), device_id_type=MESH)

    for d in range(1, nx):
        pl.semaphore_signal(barrier, inc=1, device_id=(seq, (x + d) % nx * nc + core), device_id_type=MESH)
    sibling = (seq, x * nc + (1 - core))
    pl.semaphore_signal(barrier, inc=1, device_id=sibling, device_id_type=MESH)

    def remote(src, dst, send, recv, target):
        return pltpu.make_async_remote_copy(
            src_ref=src, dst_ref=dst, send_sem=send, recv_sem=recv, device_id=target, device_id_type=MESH
        )

    own_w = pltpu.make_async_copy(w_ref, wg.at[z], own_sem.at[0])
    own_w.start()
    half = group // 2

    def ring_copy(way, r, h):
        step = 1 if way == 0 else -1
        origin = (z - step * (r - 1) + nz) % nz
        cut = pl.ds(h * half, half)
        src = w_ref.at[cut] if r == 1 else wg.at[origin, cut]
        return remote(src, wg.at[origin, cut], w_send.at[way, r - 1, h], w_recv.at[way, r - 1, h],
                      at((z + step + nz) % nz, y))

    last = (nz // 2, nz - 1 - nz // 2)

    def ring(r):
        for h in range(2):
            for way in range(2):
                if 2 <= r <= last[way] + 1:
                    ring_copy(way, r - 1, h).wait_recv()
                if r <= last[way]:
                    ring_copy(way, r, h).start()

    wide[...] = jnp.zeros_like(wide)
    for i in range(3):
        wide[3 * i:3 * i + 3, :] = taps_ref[i]
    taps = jnp.transpose(wide[...])

    lane16 = lax.broadcasted_iota(jnp.int32, (16, BLOCK), 1)
    row16 = lax.broadcasted_iota(jnp.int32, (16, BLOCK), 0)
    edge = jnp.zeros((16, OWN * nb), F32)
    for i, ref in enumerate((q_ref, k_ref, v_ref)):
        pick = ((row16 == 2 * i) & (lane16 == BLOCK - 1)) | ((row16 == 2 * i + 1) & (lane16 == BLOCK - 2))
        edge += lax.dot_general(pick.astype(F32).astype(BF16), ref[...], (((1,), (1,)), ((), ())),
                                preferred_element_type=F32)
    edge_s[...] = edge.astype(BF16)

    pad = fwd_ref.shape[0] // 2

    def spectrum():
        columns = jnp.concatenate([rows[pl.ds(c, nb, stride=OWN), :] for c in range(OWN)], axis=1)
        left = exact(fwd_ref[...], columns)
        turned = []
        for c in range(OWN):
            re, im = left[:pad, c * BLOCK:(c + 1) * BLOCK], left[pad:, c * BLOCK:(c + 1) * BLOCK]
            turned.append(jnp.concatenate([re * turn_ref[0] - im * turn_ref[1],
                                           re * turn_ref[1] + im * turn_ref[0]], axis=1))
        return exact(jnp.concatenate(turned, axis=0), rf_ref[...])

    for b in range(nb):
        rows[b * OWN:(b + 1) * OWN, :] = h_ref[:, b * BLOCK:(b + 1) * BLOCK]
    spec[...] = spectrum()

    pl.semaphore_wait(barrier, nb - 1 + nx)

    edge_copy = remote(edge_s, edge_r, edge_sem.at[0], edge_sem.at[1], ((seq + 1) % nb, tp))
    edge_copy.start()
    ring(1)
    edge_copy.wait_recv()

    wide[0:16, :] = edge_r[...].astype(F32) * jnp.where(seq > 0, 1.0, 0.0).astype(F32)
    before = jnp.transpose(wide[...])

    span = min(128, OWN * nb)
    lane = lax.broadcasted_iota(jnp.int32, (span, BLOCK), 1)
    for at_row in range(0, OWN * nb, span):
        cut = slice(at_row, at_row + span)
        shorts = []
        for i, ref in enumerate((q_ref, k_ref, v_ref)):
            now = ref[cut, :].astype(F32)
            one = jnp.where(lane == 0, before[cut, 2 * i:2 * i + 1], pltpu.roll(now, 1, 1))
            two = jnp.where(lane == 0, before[cut, 2 * i + 1:2 * i + 2],
                            jnp.where(lane == 1, before[cut, 2 * i:2 * i + 1], pltpu.roll(now, 2, 1)))
            shorts.append(taps[cut, 3 * i:3 * i + 1] * now + taps[cut, 3 * i + 1:3 * i + 2] * one
                          + taps[cut, 3 * i + 2:3 * i + 3] * two)
        pair = shorts[1] * shorts[2]
        zs_here = span // (OWN * ny)
        for yy in range(ny):
            part = jnp.concatenate([pair[(i * ny + yy) * OWN:(i * ny + yy + 1) * OWN] for i in range(zs_here)], axis=0)
            first = at_row // ny
            prod[yy, first:first + zs_here * OWN, :] = part.astype(BF16)
        for j in range(span // group):
            index = at_row // group + j
            qout[index % ny, (index // ny) * group:(index // ny + 1) * group, :] = (
                shorts[0][j * group:(j + 1) * group].astype(BF16))

    def y_copy(what, d):
        yy = (y + d) % ny
        src, dst = ((prod, yr), (qout, qr))[what]
        return remote(src.at[yy], dst.at[y], y_sem.at[what, 0, d], y_sem.at[what, 1, d], at(z, yy))

    own_y = [pltpu.make_async_copy(src.at[y], dst.at[y], own_sem.at[1 + j])
             for j, (src, dst) in enumerate(((prod, yr), (qout, qr)))]
    for what in range(2):
        own_y[what].start()
        for d in range(1, ny):
            y_copy(what, d).start()
    own_y[0].wait()
    for d in range(1, ny):
        y_copy(0, d).wait_recv()

    for zz in range(nz):
        zs[zz] = jnp.concatenate([yr[yy, pl.ds(zz * OWN // 16 * 16, 16), :].astype(F32)[zz * OWN % 16:zz * OWN % 16 + OWN]
                                  for yy in range(ny)], axis=0).astype(BF16)

    def z_copy(d):
        zz = (z + d) % nz
        return remote(zs.at[zz], xin.at[z], z_send.at[d], z_recv.at[d], at(zz, y))

    own_z = pltpu.make_async_copy(zs.at[z], xin.at[z], own_sem.at[3])
    own_z.start()

    @pl.loop(1, nz)
    def _(d):
        z_copy(d).start()

    for r in range(2, min(4, nz // 2 + 1)):
        ring(r)
    own_z.wait()

    @pl.loop(1, nz)
    def _(d):
        z_copy(d).wait_recv()

    for zz in range(nz):
        rows[zz * ny * OWN:(zz + 1) * ny * OWN, :] = xin[zz].astype(F32)
    data = spectrum()
    dr, di = data[:, :BLOCK], data[:, BLOCK:]
    fr, fi = spec[:, :BLOCK], spec[:, BLOCK:]
    mid = exact(jnp.concatenate([dr * fr - di * fi, dr * fi + di * fr], axis=1), ri_ref[...])
    turned = []
    for c in range(OWN):
        re, im = mid[c * pad:(c + 1) * pad, :BLOCK], mid[c * pad:(c + 1) * pad, BLOCK:]
        turned.append(jnp.concatenate([re * turn_ref[0] + im * turn_ref[1],
                                       im * turn_ref[0] - re * turn_ref[1]], axis=0))
    conv = exact(inv_ref[...], jnp.concatenate(turned, axis=1))
    for c in range(OWN):
        rows[pl.ds(c, nb, stride=OWN), :] = conv[:, c * BLOCK:(c + 1) * BLOCK]
    for zz in range(nz):
        ms[zz] = rows[zz * ny * OWN:(zz + 1) * ny * OWN, :].astype(BF16)

    to_y = z // 2 % ny
    my_slot = ((z // (2 * ny)) * 2 + z % 2) * ny + y

    def c_copy(d):
        zz = (z + d) % nz
        return remote(ms.at[zz], ar.at[my_slot], c_send.at[d], c_recv.at[my_slot], at(zz, to_y))

    @pl.loop(1, nz)
    def _(d):
        c_copy(d).start()

    here = pltpu.make_async_copy(ms.at[z], ar.at[my_slot], c_recv.at[my_slot])

    @pl.when(to_y == y)
    def _():
        here.start()

    @pl.when(to_y != y)
    def _():
        c_copy(0).start()

    for r in range(4, min(6, nz // 2 + 1)):
        ring(r)
    own_y[1].wait()
    for d in range(1, ny):
        y_copy(1, d).wait_recv()

    @pl.loop(0, nz)
    def _(slot):
        pltpu.make_async_copy(ms.at[0], ar.at[slot], c_recv.at[slot]).wait()

    for yy in range(ny):
        part = []
        for slot in range(nz):
            got = ar[slot, yy * OWN // 16 * 16:yy * OWN // 16 * 16 + 16, :].astype(F32)
            part.append(got[yy * OWN % 16:yy * OWN % 16 + OWN])
        mixed = jnp.concatenate(part, axis=0)
        gated = qr[yy].astype(F32) * mixed
        if nz * OWN < BLOCK:
            gated = jnp.concatenate([gated] * (BLOCK // (nz * OWN)), axis=0)
        gt[yy * BLOCK:(yy + 1) * BLOCK, :] = jnp.transpose(gated).astype(BF16)

    def x_copy(d):
        xx = (x + d) % nx
        return remote(gt, ga.at[tp], x_send.at[d], x_recv.at[d], (seq, xx * nc + core))

    def b_copy(d):
        slot = (x - d + nx) % nx * nc + core
        return remote(gt if d == 0 else ga.at[slot], ga.at[slot], b_send.at[d], b_recv.at[d], sibling)

    own_g = pltpu.make_async_copy(gt, ga.at[tp], own_sem.at[4])
    for d in range(1, nx):
        x_copy(d).start()
    b_copy(0).start()
    own_g.start()
    for r in range(6, nz // 2 + 2):
        ring(r)
    if nz // 2 + 2 <= 6:
        for r in range(min(6, nz // 2 + 1), nz // 2 + 2):
            ring(r)
    for d in range(1, nx):
        x_copy(d).wait_recv()
        b_copy(d).start()
    own_g.wait()
    own_w.wait()
    for d in range(nx):
        b_copy(d).wait_recv()

    depth = nz * OWN
    columns = out_ref.shape[1]
    tile = min(256, columns)

    def partial_sum(yy, start):
        lhs = jnp.concatenate([ga[p, pl.ds(pl.multiple_of(yy * BLOCK, BLOCK), BLOCK), :][:, :depth] for p in range(ntp)],
                              axis=1)
        return jnp.dot(lhs, wg[:, :, pl.ds(start, tile)].reshape(nz * group, tile), preferred_element_type=F32)

    def r_copy(d):
        return remote(ps.at[d], pr.at[d], r_send.at[d], r_recv.at[d], at(z, (y + d) % ny))

    for d in list(range(1, ny)):
        @pl.loop(0, columns // tile)
        def _(n):
            start = pl.multiple_of(n * tile, tile)
            ps[d, :, pl.ds(start, tile)] = partial_sum((y + d) % ny, start).astype(BF16)
        r_copy(d).start()

    @pl.loop(0, columns // tile)
    def _(n):
        start = pl.multiple_of(n * tile, tile)
        total[:, pl.ds(start, tile)] = partial_sum(y, start)

    for d in range(1, ny):
        r_copy(d).wait_recv()
    sums = total[...]
    for d in range(1, ny):
        sums += pr[d].astype(F32)
    out_ref[...] = sums.astype(BF16)

    edge_copy.wait_send()
    for way in range(2):
        for r in range(1, last[way] + 1):
            for h in range(2):
                ring_copy(way, r, h).wait_send()
    for what in range(2):
        for d in range(1, ny):
            y_copy(what, d).wait_send()

    @pl.loop(1, nz)
    def _(d):
        z_copy(d).wait_send()
        c_copy(d).wait_send()

    @pl.when(to_y != y)
    def _():
        c_copy(0).wait_send()

    for d in range(1, nx):
        x_copy(d).wait_send()
    for d in range(nx):
        b_copy(d).wait_send()
    for d in range(1, ny):
        r_copy(d).wait_send()


def build(mesh, nz, ny, nx):
    nb, ntp = nz * ny, nx * 2
    held = OWN * nb
    group = OWN * ntp
    consts = tables(nb)

    def shards(query_proj, key_proj, value_proj, short_taps, long_filters, out_weight):
        columns = out_weight.shape[1]
        pad = consts[0].shape[0] // 2
        dma = pltpu.SemaphoreType.DMA
        vmem = pltpu.VMEM
        return pl.pallas_call(
            functools.partial(kernel, nz, ny, nx),
            out_shape=jax.ShapeDtypeStruct((BLOCK, columns), BF16),
            in_specs=[pl.BlockSpec(memory_space=pltpu.VMEM)] * 11,
            out_specs=pl.BlockSpec(memory_space=pltpu.VMEM),
            scratch_shapes=[
                vmem((BLOCK, held), F32),
                vmem((16, held), BF16),
                vmem((16, held), BF16),
                vmem((ny, nz * OWN, BLOCK), BF16),
                vmem((ny, nz * OWN, BLOCK), BF16),
                vmem((ny, nz * OWN, BLOCK), BF16),
                vmem((ny, nz * OWN, BLOCK), BF16),
                vmem((nz, ny * OWN, BLOCK), BF16),
                vmem((nz, ny * OWN, BLOCK), BF16),
                vmem((held, BLOCK), F32),
                vmem((OWN * pad, 2 * BLOCK), F32),
                vmem((nz, ny * OWN, BLOCK), BF16),
                vmem((nz, ny * OWN, BLOCK), BF16),
                vmem((ny * BLOCK, BLOCK), BF16),
                vmem((ntp, ny * BLOCK, BLOCK), BF16),
                vmem((nz, group, columns), BF16),
                vmem((ny, BLOCK, columns), BF16),
                vmem((ny, BLOCK, columns), BF16),
                vmem((BLOCK, columns), F32),
                dma((2,)),
                dma((2, 2, ny)),
                dma((nz,)),
                dma((nz,)),
                dma((nz,)),
                dma((nz,)),
                dma((nx,)),
                dma((nx,)),
                dma((nx,)),
                dma((nx,)),
                dma((2, nz // 2, 2)),
                dma((2, nz // 2, 2)),
                dma((ny,)),
                dma((ny,)),
                dma((5,)),
            ],
            compiler_params=pltpu.CompilerParams(
                collective_id=0, has_side_effects=True, vmem_limit_bytes=60 * 1024 * 1024
            ),
        )(query_proj, key_proj, value_proj, short_taps, long_filters, out_weight, *[jnp.asarray(a) for a in consts])

    return jax.shard_map(
        shards,
        mesh=mesh,
        in_specs=(
            P("tp", "seq"),
            P("tp", "seq"),
            P("tp", "seq"),
            P(None, None, "tp"),
            P(("tp", "seq"), None),
            P("seq", "tp"),
        ),
        out_specs=P("seq", "tp"),
        check_vma=False,
    )


def solution(mesh):
    return build(mesh, mesh.shape["seq"] // 4, 4, mesh.shape["tp"] // 2)
```

time: 293 us -> 85.7 us (0.29)
  the two profiles are of different devices: /device:TPU:6 before, /device:TPU:1 now
where the time goes in v1:
time: 85.7 us; the launch traced here: 85.6 us
  Pallas kernels  83.9 us (98%)
  local copies, waits for them, and re-layouts  1.67 us (2%)
    pallas_call x1, Pallas kernels, shards(): pl.pallas_call(functools.partial(kernel, nz, ny, nx), out_shape=jax.Shape...  83.9 us

profile of v1, /device:TPU:1, one launch (start us, length us, event | category | flops | bytes accessed | tf_op | source)
XLA Modules:
  0.0 85.6 jit_solution(4398918910713392213)
XLA Ops:
  0.0 83.9 %shard_map.109 = bf16[128,1024]{1,0:T(8,128)(2,1)} custom-call(bf16[512,128]{1,0:T(8,128)(2,1)} %q_ref.1, bf16[512,128]{1,0:T(8,128)(2,1)} %k_ref.1, bf16[512,128]{1,0:T(8,128)(2,1)} %v_ref.1, f32[3,3,512]{2,1,0:T(4,128)} %taps_ref.1, f32[8,8192]{1,0:T(8,128)} %h_ref.1, bf16[64,1024]{1,0:T(8,128)(2,1)} %w_ref.1, f32[144,64]{1,0:T(8,128)} %constant.10.clone.fwd_ref, ...), custom_call_target="tpu_custom_call" | custom-call | tf_op jit(solution)/shard_map/pallas_call | solution.py:351
  83.9 1.7 %copy.13 = bf16[128,1024]{1,0:T(8,128)(2,1)} copy(bf16[128,1024]{1,0:T(8,128)(2,1)} %shard_map.109) | data formatting | bytes 524288

commit v2 on v1

v2 whole, which is shorter than its diff:
```python
import functools
import math

import jax
import jax.numpy as jnp
import numpy as np
from jax import lax
from jax.experimental import pallas as pl
from jax.experimental.pallas import tpu as pltpu
from jax.sharding import PartitionSpec as P

MESH = pl.DeviceIdType.MESH
F32 = jnp.float32
BF16 = jnp.bfloat16
BLOCK = 128
OWN = 8
exact = functools.partial(jnp.dot, precision=lax.Precision.HIGHEST, preferred_element_type=F32)


def tables(blocks):
    period = 2 * blocks * BLOCK
    padded = -(-(blocks + 1) // 8) * 8
    kb = np.arange(padded)[:, None]
    live = kb <= blocks
    left = 2 * math.pi * (kb * np.arange(blocks)[None, :] % (2 * blocks)) / (2 * blocks)
    forward = np.concatenate([live * np.cos(left), -(live * np.sin(left))], axis=0)
    share = np.where((kb == 0) | (kb == blocks), 1.0, 2.0) * live / period
    inverse = np.concatenate([share * np.cos(left), -(share * np.sin(left))], axis=0).T
    twist = 2 * math.pi * (kb * np.arange(BLOCK)[None, :] % period) / period
    turn = np.stack([np.cos(twist), -np.sin(twist)])
    right = np.arange(BLOCK)
    right = 2 * math.pi * (right[:, None] * right[None, :] % BLOCK) / BLOCK
    c, s = np.cos(right), np.sin(right)
    rows = np.block([[c, -s], [s, c]])
    return [np.asarray(a, np.float32) for a in (forward, inverse, turn, rows, np.ascontiguousarray(rows.T))]


def kernel(
    nz, ny, nx,
    q_ref, k_ref, v_ref, taps_ref, h_ref, w_ref,
    fwd_ref, inv_ref, turn_ref, rf_ref, ri_ref,
    out_ref,
    wide, tapst, edge_s, edge_r, raw, got, qs, zs, xin, rows, spec, ms, ar, ga, wp, wg, ps, half_r, pr, total,
    e_sem, y_send, y_recv, wy_send, wy_recv, z_send, z_recv, c_send, c_recv, x_send, x_recv, b_send, b_recv,
    w_send, w_recv, r_send, r_recv, own_sem,
):
    nc = 2
    nb = nz * ny
    ntp = nx * nc
    held = nz * OWN
    seq = lax.axis_index("seq")
    tp = lax.axis_index("tp")
    z, y = seq // ny, seq % ny
    x, core = tp // nc, tp % nc

    def at(zz, yy):
        return (zz * ny + yy, tp)

    def along(d):
        return (seq, (x + d + nx) % nx * nc + core)

    barrier = pltpu.get_barrier_semaphore()
    sibling = (seq, x * nc + (1 - core))

    def greet(target):
        pl.semaphore_signal(barrier, inc=1, device_id=target, device_id_type=MESH)

    @pl.loop(1, nz)
    def _(d):
        greet(at((z + d) % nz, y))

    greet(at((z + nz - 1) % nz, ny - 1))
    for d in range(1, ny):
        greet(at(z, (y + d) % ny))
    for d in range(1, nx):
        greet(along(d))
    greet(sibling)

    def remote(src, dst, send, recv, target):
        return pltpu.make_async_remote_copy(
            src_ref=src, dst_ref=dst, send_sem=send, recv_sem=recv, device_id=target, device_id_type=MESH
        )

    def ring_copy(way, r, h):
        step = 1 if way == 0 else -1
        origin = (z - step * (r - 1) + nz) % nz
        piece = wg.at[origin, pl.ds(h * (ny // 2), ny // 2)]
        return remote(piece, piece, w_send.at[way, r - 1, h], w_recv.at[way, r - 1, h], at((z + step + nz) % nz, y))

    last = (nz // 2, nz - 1 - nz // 2)

    def ring(r):
        for h in range(2):
            for way in range(2):
                if 2 <= r <= last[way] + 1:
                    ring_copy(way, r - 1, h).wait_recv()
                if r <= last[way]:
                    ring_copy(way, r, h).start()

    streams = (q_ref, k_ref, v_ref)
    lane16 = lax.broadcasted_iota(jnp.int32, (16, BLOCK), 1)
    row16 = lax.broadcasted_iota(jnp.int32, (16, BLOCK), 0)
    for yy in range(ny):
        edge = jnp.zeros((16, held), F32)
        for i, ref in enumerate(streams):
            part = jnp.concatenate(
                [ref[(zz * ny + yy) * OWN // 16 * 16:(zz * ny + yy) * OWN // 16 * 16 + 16, :].astype(F32)
                 [(zz * ny + yy) * OWN % 16:(zz * ny + yy) * OWN % 16 + OWN] for zz in range(nz)], axis=0).astype(BF16)
            raw[i, yy] = part
            pick = ((row16 == 2 * i) & (lane16 == BLOCK - 1)) | ((row16 == 2 * i + 1) & (lane16 == BLOCK - 2))
            edge += lax.dot_general(pick.astype(F32).astype(BF16), part, (((1,), (1,)), ((), ())),
                                    preferred_element_type=F32)
        edge_s[yy] = edge.astype(BF16)
    wide[...] = jnp.zeros_like(wide)
    for i in range(3):
        wide[3 * i:3 * i + 3, :] = taps_ref[i]
    tapst[...] = jnp.transpose(wide[...])
    taps = jnp.concatenate(
        [tapst[pl.ds(pl.multiple_of((zz * ny + y) * OWN, OWN), OWN), :] for zz in range(nz)], axis=0)
    piece = wp.shape[1]
    for yy in range(ny):
        wp[yy] = jnp.concatenate(
            [w_ref[j * OWN // 16 * 16:j * OWN // 16 * 16 + 16, :].astype(F32)[j * OWN % 16:j * OWN % 16 + OWN]
             for j in range(yy, ntp, ny)], axis=0).astype(BF16)

    pad = fwd_ref.shape[0] // 2

    def spectrum():
        columns = jnp.concatenate([rows[pl.ds(c, nb, stride=OWN), :] for c in range(OWN)], axis=1)
        left = exact(fwd_ref[...], columns)
        turned = []
        for c in range(OWN):
            re, im = left[:pad, c * BLOCK:(c + 1) * BLOCK], left[pad:, c * BLOCK:(c + 1) * BLOCK]
            turned.append(jnp.concatenate([re * turn_ref[0] - im * turn_ref[1],
                                           re * turn_ref[1] + im * turn_ref[0]], axis=1))
        return exact(jnp.concatenate(turned, axis=0), rf_ref[...])

    for b in range(nb):
        rows[b * OWN:(b + 1) * OWN, :] = h_ref[:, b * BLOCK:(b + 1) * BLOCK]
    spec[...] = spectrum()

    pl.semaphore_wait(barrier, nz - 1 + 1 - 1 + ny - 1 + nx - 1 + 1 + jnp.where(y == ny - 1, ny, 0))

    def y_copy(i, d):
        yy = (y + d) % ny
        return remote(raw.at[i, yy], got.at[i, y], y_send.at[i, d], y_recv.at[i, d], at(z, yy))

    def edge_copy(yy):
        return remote(edge_s.at[yy], edge_r, e_sem.at[1 + yy], e_sem.at[0], at((z + 1) % nz, yy))

    def wy_copy(d):
        yy = (y + d) % ny
        return remote(wp.at[yy], wg.at[z, y], wy_send.at[d], wy_recv.at[d], at(z, yy))

    own_y = [pltpu.make_async_copy(raw.at[i, y], got.at[i, y], own_sem.at[i]) for i in range(3)]
    own_w = pltpu.make_async_copy(wp.at[y], wg.at[z, y], own_sem.at[3])
    far = list(range(2, ny - 1)) + [1, ny - 1]

    @pl.when(y == ny - 1)
    def _():
        for yy in range(ny):
            edge_copy(yy).start()

    for i in (1, 2, 0):
        for d in far:
            y_copy(i, d).start()
        own_y[i].start()
    for d in far:
        wy_copy(d).start()
    own_w.start()

    lane = lax.broadcasted_iota(jnp.int32, (held, BLOCK), 1)
    edge_copy(0).wait_recv()
    wide[0:16, 0:held] = edge_r[...].astype(F32) * jnp.where(z > 0, 1.0, 0.0).astype(F32)
    before = jnp.transpose(wide[:, 0:held])

    def short(i):
        own_y[i].wait()
        for d in range(1, ny):
            y_copy(i, d).wait_recv()
        ahead1 = jnp.where(lane == 0, before[:, 2 * i:2 * i + 1], 0.0)
        ahead2 = jnp.where(lane == 0, before[:, 2 * i + 1:2 * i + 2],
                           jnp.where(lane == 1, before[:, 2 * i:2 * i + 1], 0.0))
        result = []
        for b in range(ny):
            now = got[i, b].astype(F32)
            roll1, roll2 = pltpu.roll(now, 1, 1), pltpu.roll(now, 2, 1)
            one = jnp.where(lane == 0, ahead1, roll1)
            two = jnp.where(lane < 2, ahead2, roll2)
            result.append(taps[:, 3 * i:3 * i + 1] * now + taps[:, 3 * i + 1:3 * i + 2] * one
                          + taps[:, 3 * i + 2:3 * i + 3] * two)
            ahead1, ahead2 = roll1, roll2
        return result

    pair = [a * c for a, c in zip(short(1), short(2))]
    for zz in range(nz):
        zs[zz] = jnp.concatenate([pair[b][zz * OWN:(zz + 1) * OWN] for b in range(ny)], axis=0).astype(BF16)

    def z_copy(d):
        zz = (z + d) % nz
        return remote(zs.at[zz], xin.at[z], z_send.at[d], z_recv.at[d], at(zz, y))

    own_z = pltpu.make_async_copy(zs.at[z], xin.at[z], own_sem.at[4])

    @pl.loop(1, nz)
    def _(d):
        z_copy(d).start()

    own_z.start()
    own_w.wait()
    for d in range(1, ny):
        wy_copy(d).wait_recv()
    ring(1)
    for b, value in enumerate(short(0)):
        qs[b] = value
    for r in range(2, min(3, nz // 2 + 1)):
        ring(r)
    own_z.wait()

    @pl.loop(1, nz)
    def _(d):
        z_copy(d).wait_recv()

    for zz in range(nz):
        rows[zz * ny * OWN:(zz + 1) * ny * OWN, :] = xin[zz].astype(F32)
    data = spectrum()
    for r in range(3, min(4, nz // 2 + 1)):
        ring(r)
    dr, di = data[:, :BLOCK], data[:, BLOCK:]
    fr, fi = spec[:, :BLOCK], spec[:, BLOCK:]
    mid = exact(jnp.concatenate([dr * fr - di * fi, dr * fi + di * fr], axis=1), ri_ref[...])
    turned = []
    for c in range(OWN):
        re, im = mid[c * pad:(c + 1) * pad, :BLOCK], mid[c * pad:(c + 1) * pad, BLOCK:]
        turned.append(jnp.concatenate([re * turn_ref[0] + im * turn_ref[1],
                                       im * turn_ref[0] - re * turn_ref[1]], axis=0))
    conv = exact(inv_ref[...], jnp.concatenate(turned, axis=1))
    for c in range(OWN):
        rows[pl.ds(c, nb, stride=OWN), :] = conv[:, c * BLOCK:(c + 1) * BLOCK]
    for zz in range(nz):
        ms[zz] = rows[zz * ny * OWN:(zz + 1) * ny * OWN, :].astype(BF16)

    def c_copy(d):
        zz = (z + d) % nz
        return remote(ms.at[zz], ar.at[z], c_send.at[d], c_recv.at[d], at(zz, y))

    own_c = pltpu.make_async_copy(ms.at[z], ar.at[z], own_sem.at[5])

    @pl.loop(1, nz)
    def _(d):
        c_copy(d).start()

    own_c.start()
    for r in range(4, min(6, nz // 2 + 1)):
        ring(r)
    own_c.wait()

    @pl.loop(1, nz)
    def _(d):
        c_copy(d).wait_recv()

    order = [(y + d) % ny for d in (2, 1, 3, 0)]

    def slot(d):
        return (x - d + nx) % nx * nc + core

    def x_copy(d, i):
        b = order[i]
        if d != 2:
            return remote(ga.at[tp, b], ga.at[tp, b], x_send.at[d, i], x_recv.at[d, i], along(d))
        origin, step = (slot(1), 1) if i % 2 == 0 else (slot(3), -1)
        return remote(ga.at[origin, b], ga.at[origin, b], x_send.at[d, i], x_recv.at[d, i], along(step))

    def b_copy(d, i):
        b = order[i]
        return remote(ga.at[slot(d), b], ga.at[slot(d), b], b_send.at[d, i], b_recv.at[d, i], sibling)

    depth = held
    columns = out_ref.shape[1]
    tiles, tile = total.shape[0], total.shape[2]

    def gate(i):
        b = order[i]
        mixed = jnp.concatenate(
            [rows[pl.ds(pl.multiple_of((zz * ny + b) * OWN, OWN), OWN), :] for zz in range(nz)], axis=0)
        gated = qs[b] * mixed
        if held < BLOCK:
            gated = jnp.concatenate([gated] * (BLOCK // held), axis=0)
        ga[tp, b] = jnp.transpose(gated).astype(BF16)
        for d in (1, 3):
            x_copy(d, i).start()
        b_copy(0, i).start()

    def relay(i):
        for d in (1, 3):
            x_copy(d, i).wait_recv()
        x_copy(2, i).start()
        for d in (1, 3):
            b_copy(d, i).start()

    def settle(i):
        x_copy(2, i).wait_recv()
        b_copy(2, i).start()
        for d in range(nx):
            b_copy(d, i).wait_recv()

    def partial_sum(i, n):
        lhs = jnp.concatenate([ga[p, order[i]][:, :depth] for p in range(ntp)], axis=1)
        rhs = wg[:, :, :, pl.ds(pl.multiple_of(n * tile, tile), tile)].reshape(ntp * depth, tile)
        return jnp.dot(lhs, rhs, preferred_element_type=F32)

    def half_copy(h):
        return remote(ps.at[0, pl.ds(h * (tiles // 2), tiles // 2)], half_r.at[h], r_send.at[h], r_recv.at[h],
                      at(z, (y + (1, ny - 1)[h]) % ny))

    def r_copy(h):
        return remote(ps.at[1 + h], pr.at[h], r_send.at[2 + h], r_recv.at[2 + h], at(z, (y + (1, ny - 1)[h]) % ny))

    for zz in range(nz):
        rows[zz * ny * OWN:(zz + 1) * ny * OWN, :] = ar[zz].astype(F32)

    gate(0)
    gate(1)
    for r in range(6, min(7, nz // 2 + 1)):
        ring(r)
    relay(0)
    gate(2)
    relay(1)
    gate(3)
    for r in range(7, min(8, nz // 2 + 1)):
        ring(r)
    settle(0)
    relay(2)
    for r in range(8, min(9, nz // 2 + 1)):
        ring(r)
    settle(1)
    relay(3)
    ring(nz // 2 + 1)

    @pl.loop(0, tiles)
    def _(n):
        ps[0, n] = partial_sum(0, n).astype(BF16)

    for h in range(2):
        half_copy(h).start()

    for h in range(2):
        if h == 1:
            settle(2)
        @pl.loop(0, tiles)
        def _(n):
            total[n] = partial_sum(1 + h, n)
        half_copy(h).wait_recv()
        for n in range(tiles):
            if n // (tiles // 2) == h:
                ps[1 + h, n] = (total[n] + half_r[h, n % (tiles // 2)].astype(F32)).astype(BF16)
            else:
                ps[1 + h, n] = total[n].astype(BF16)
        r_copy(h).start()

    settle(3)

    @pl.loop(0, tiles)
    def _(n):
        total[n] = partial_sum(3, n)

    for h in range(2):
        r_copy(h).wait_recv()
    for n in range(tiles):
        out_ref[:, n * tile:(n + 1) * tile] = (total[n] + pr[0, n].astype(F32) + pr[1, n].astype(F32)).astype(BF16)

    @pl.when(y == ny - 1)
    def _():
        for yy in range(ny):
            edge_copy(yy).wait_send()

    for way in range(2):
        for r in range(1, last[way] + 1):
            for h in range(2):
                ring_copy(way, r, h).wait_send()
    for d in range(1, ny):
        for i in range(3):
            y_copy(i, d).wait_send()
        wy_copy(d).wait_send()

    @pl.loop(1, nz)
    def _(d):
        z_copy(d).wait_send()
        c_copy(d).wait_send()

    for i in range(ny):
        for d in range(1, nx):
            x_copy(d, i).wait_send()
        for d in range(nx):
            b_copy(d, i).wait_send()
    for h in range(2):
        half_copy(h).wait_send()
        r_copy(h).wait_send()


def build(mesh, nz, ny, nx):
    nb, ntp = nz * ny, nx * 2
    held = OWN * nb
    group = OWN * ntp
    consts = tables(nb)

    def shards(query_proj, key_proj, value_proj, short_taps, long_filters, out_weight):
        columns = out_weight.shape[1]
        tile = min(256, columns // 2)
        pad = consts[0].shape[0] // 2
        dma = pltpu.SemaphoreType.DMA
        vmem = pltpu.VMEM
        return pl.pallas_call(
            functools.partial(kernel, nz, ny, nx),
            out_shape=jax.ShapeDtypeStruct((BLOCK, columns), BF16),
            in_specs=[pl.BlockSpec(memory_space=pltpu.VMEM)] * 11,
            out_specs=pl.BlockSpec(memory_space=pltpu.VMEM),
            scratch_shapes=[
                vmem((BLOCK, held), F32),
                vmem((held, BLOCK), F32),
                vmem((ny, 16, nz * OWN), BF16),
                vmem((16, nz * OWN), BF16),
                vmem((3, ny, nz * OWN, BLOCK), BF16),
                vmem((3, ny, nz * OWN, BLOCK), BF16),
                vmem((ny, nz * OWN, BLOCK), F32),
                vmem((nz, ny * OWN, BLOCK), BF16),
                vmem((nz, ny * OWN, BLOCK), BF16),
                vmem((held, BLOCK), F32),
                vmem((OWN * pad, 2 * BLOCK), F32),
                vmem((nz, ny * OWN, BLOCK), BF16),
                vmem((nz, ny * OWN, BLOCK), BF16),
                vmem((ntp, ny, BLOCK, BLOCK), BF16),
                vmem((ny, group // ny, columns), BF16),
                vmem((nz, ny, group // ny, columns), BF16),
                vmem((3, columns // tile, BLOCK, tile), BF16),
                vmem((2, columns // tile // 2, BLOCK, tile), BF16),
                vmem((2, columns // tile, BLOCK, tile), BF16),
                vmem((columns // tile, BLOCK, tile), F32),
                dma((1 + ny,)),
                dma((3, ny)),
                dma((3, ny)),
                dma((ny,)),
                dma((ny,)),
                dma((nz,)),
                dma((nz,)),
                dma((nz,)),
                dma((nz,)),
                dma((nx, ny)),
                dma((nx, ny)),
                dma((nx, ny)),
                dma((nx, ny)),
                dma((2, nz // 2, 2)),
                dma((2, nz // 2, 2)),
                dma((4,)),
                dma((4,)),
                dma((6,)),
            ],
            compiler_params=pltpu.CompilerParams(
                collective_id=0, has_side_effects=True, vmem_limit_bytes=60 * 1024 * 1024
            ),
        )(query_proj, key_proj, value_proj, short_taps, long_filters, out_weight, *[jnp.asarray(a) for a in consts])

    return jax.shard_map(
        shards,
        mesh=mesh,
        in_specs=(
            P("tp", "seq"),
            P("tp", "seq"),
            P("tp", "seq"),
            P(None, None, "tp"),
            P(("tp", "seq"), None),
            P("seq", "tp"),
        ),
        out_specs=P("seq", "tp"),
        check_vma=False,
    )


def solution(mesh):
    return build(mesh, mesh.shape["seq"] // 4, 4, mesh.shape["tp"] // 2)
```

time: 85.7 us -> 83.9 us (0.979)
  Pallas kernels: 83.9 us -> 82.1 us
    pallas_call x1, Pallas kernels: 83.9 us -> 82.1 us  [shards(): pl.pallas_call(functools.partial(kernel, nz, ny, nx), out_shape=jax.Shape...]
where the time goes in v2:
time: 83.9 us; the launch traced here: 83.8 us
  Pallas kernels  82.1 us (98%)
  local copies, waits for them, and re-layouts  1.67 us (2%)
    pallas_call x1, Pallas kernels, shards(): pl.pallas_call(functools.partial(kernel, nz, ny, nx), out_shape=jax.Shape...  82.1 us

profile of v2, /device:TPU:1, one launch (start us, length us, event | category | flops | bytes accessed | tf_op | source)
XLA Modules:
  0.0 83.8 jit_solution(4787107730534578200)
XLA Ops:
  0.0 82.1 %shard_map.109 = bf16[128,1024]{1,0:T(8,128)(2,1)} custom-call(bf16[512,128]{1,0:T(8,128)(2,1)} %q_ref.1, bf16[512,128]{1,0:T(8,128)(2,1)} %k_ref.1, bf16[512,128]{1,0:T(8,128)(2,1)} %v_ref.1, f32[3,3,512]{2,1,0:T(4,128)} %taps_ref.1, f32[8,8192]{1,0:T(8,128)} %h_ref.1, bf16[64,1024]{1,0:T(8,128)(2,1)} %w_ref.1, f32[144,64]{1,0:T(8,128)} %constant.10.clone.fwd_ref, ...), custom_call_target="tpu_custom_call" | custom-call | tf_op jit(solution)/shard_map/pallas_call | solution.py:413
  82.1 1.7 %copy.13 = bf16[128,1024]{1,0:T(8,128)(2,1)} copy(bf16[128,1024]{1,0:T(8,128)(2,1)} %shard_map.109) | data formatting | bytes 524288

commit v3 on v2

--- a/solution.py
+++ b/solution.py
@@ -42,7 +42,7 @@
     out_ref,
     wide, tapst, edge_s, edge_r, raw, got, qs, zs, xin, rows, spec, ms, ar, ga, wp, wg, ps, half_r, pr, total,
     e_sem, y_send, y_recv, wy_send, wy_recv, z_send, z_recv, c_send, c_recv, x_send, x_recv, b_send, b_recv,
-    w_send, w_recv, r_send, r_recv, own_sem,
+    w_send, w_recv, r_send, r_recv, own_sem, ready,
 ):
     nc = 2
     nb = nz * ny
@@ -65,10 +65,8 @@
     def greet(target):
         pl.semaphore_signal(barrier, inc=1, device_id=target, device_id_type=MESH)
 
-    @pl.loop(1, nz)
-    def _(d):
+    for d in (1, nz - 1):
         greet(at((z + d) % nz, y))
-
     greet(at((z + nz - 1) % nz, ny - 1))
     for d in range(1, ny):
         greet(at(z, (y + d) % ny))
@@ -139,7 +137,20 @@
         rows[b * OWN:(b + 1) * OWN, :] = h_ref[:, b * BLOCK:(b + 1) * BLOCK]
     spec[...] = spectrum()
 
-    pl.semaphore_wait(barrier, nz - 1 + 1 - 1 + ny - 1 + nx - 1 + 1 + jnp.where(y == ny - 1, ny, 0))
+    pl.semaphore_wait(barrier, 2 + ny - 1 + nx - 1 + 1 + jnp.where(y == ny - 1, ny, 0))
+
+    def word(r):
+        if 2 <= r <= nz // 2:
+            for way in range(2):
+                if r > 2:
+                    pl.semaphore_wait(ready.at[way, r - 1], 1)
+                pl.semaphore_signal(ready.at[way, r], inc=1, device_id=at((z + (1, nz - 1)[way]) % nz, y),
+                                    device_id_type=MESH)
+
+    def heard():
+        if nz // 2 >= 2:
+            for way in range(2):
+                pl.semaphore_wait(ready.at[way, nz // 2], 1)
 
     def y_copy(i, d):
         yy = (y + d) % ny
@@ -155,19 +166,28 @@
     own_y = [pltpu.make_async_copy(raw.at[i, y], got.at[i, y], own_sem.at[i]) for i in range(3)]
     own_w = pltpu.make_async_copy(wp.at[y], wg.at[z, y], own_sem.at[3])
     far = list(range(2, ny - 1)) + [1, ny - 1]
+
+    word(2)
 
     @pl.when(y == ny - 1)
     def _():
         for yy in range(ny):
             edge_copy(yy).start()
 
+    for d in far:
+        wy_copy(d).start()
     for i in (1, 2, 0):
         for d in far:
             y_copy(i, d).start()
+    own_w.start()
+    for i in (1, 2, 0):
         own_y[i].start()
-    for d in far:
-        wy_copy(d).start()
-    own_w.start()
+    word(3)
+    own_w.wait()
+    for d in range(1, ny):
+        wy_copy(d).wait_recv()
+    ring(1)
+    word(4)
 
     lane = lax.broadcasted_iota(jnp.int32, (held, BLOCK), 1)
     edge_copy(0).wait_recv()
@@ -192,7 +212,15 @@
             ahead1, ahead2 = roll1, roll2
         return result
 
-    pair = [a * c for a, c in zip(short(1), short(2))]
+    key_short = short(1)
+    word(5)
+    word(6)
+    value_short = short(2)
+    word(7)
+    word(8)
+    for r in range(9, nz // 2 + 1):
+        word(r)
+    pair = [a * c for a, c in zip(key_short, value_short)]
     for zz in range(nz):
         zs[zz] = jnp.concatenate([pair[b][zz * OWN:(zz + 1) * OWN] for b in range(ny)], axis=0).astype(BF16)
 
@@ -200,6 +228,7 @@
         zz = (z + d) % nz
         return remote(zs.at[zz], xin.at[z], z_send.at[d], z_recv.at[d], at(zz, y))
 
+    heard()
     own_z = pltpu.make_async_copy(zs.at[z], xin.at[z], own_sem.at[4])
 
     @pl.loop(1, nz)
@@ -207,13 +236,11 @@
         z_copy(d).start()
 
     own_z.start()
-    own_w.wait()
-    for d in range(1, ny):
-        wy_copy(d).wait_recv()
-    ring(1)
+    for r in range(2, min(3, nz // 2 + 1)):
+        ring(r)
     for b, value in enumerate(short(0)):
         qs[b] = value
-    for r in range(2, min(3, nz // 2 + 1)):
+    for r in range(3, min(4, nz // 2 + 1)):
         ring(r)
     own_z.wait()
 
@@ -223,9 +250,9 @@
 
     for zz in range(nz):
         rows[zz * ny * OWN:(zz + 1) * ny * OWN, :] = xin[zz].astype(F32)
+    for r in range(4, min(5, nz // 2 + 1)):
+        ring(r)
     data = spectrum()
-    for r in range(3, min(4, nz // 2 + 1)):
-        ring(r)
     dr, di = data[:, :BLOCK], data[:, BLOCK:]
     fr, fi = spec[:, :BLOCK], spec[:, BLOCK:]
     mid = exact(jnp.concatenate([dr * fr - di * fi, dr * fi + di * fr], axis=1), ri_ref[...])
@@ -251,7 +278,7 @@
         c_copy(d).start()
 
     own_c.start()
-    for r in range(4, min(6, nz // 2 + 1)):
+    for r in range(5, min(7, nz // 2 + 1)):
         ring(r)
     own_c.wait()
 
@@ -313,16 +340,17 @@
         return remote(ps.at[0, pl.ds(h * (tiles // 2), tiles // 2)], half_r.at[h], r_send.at[h], r_recv.at[h],
                       at(z, (y + (1, ny - 1)[h]) % ny))
 
-    def r_copy(h):
-        return remote(ps.at[1 + h], pr.at[h], r_send.at[2 + h], r_recv.at[2 + h], at(z, (y + (1, ny - 1)[h]) % ny))
+    def r_copy(h, late):
+        cut = pl.ds((h if late else 1 - h) * (tiles // 2), tiles // 2)
+        k = 2 + 2 * h + late
+        return remote(ps.at[1 + h, cut], pr.at[h, cut], r_send.at[k], r_recv.at[k],
+                      at(z, (y + (1, ny - 1)[h]) % ny))
 
     for zz in range(nz):
         rows[zz * ny * OWN:(zz + 1) * ny * OWN, :] = ar[zz].astype(F32)
 
     gate(0)
     gate(1)
-    for r in range(6, min(7, nz // 2 + 1)):
-        ring(r)
     relay(0)
     gate(2)
     relay(1)
@@ -344,19 +372,24 @@
     for h in range(2):
         half_copy(h).start()
 
+    half = tiles // 2
     for h in range(2):
         if h == 1:
             settle(2)
-        @pl.loop(0, tiles)
+
+        @pl.loop((1 - h) * half, (1 - h) * half + half)
         def _(n):
-            total[n] = partial_sum(1 + h, n)
+            ps[1 + h, n] = partial_sum(1 + h, n).astype(BF16)
+        r_copy(h, 0).start()
+
+    for h in range(2):
+        @pl.loop(0, half)
+        def _(n):
+            total[h * half + n] = partial_sum(1 + h, h * half + n)
         half_copy(h).wait_recv()
-        for n in range(tiles):
-            if n // (tiles // 2) == h:
-                ps[1 + h, n] = (total[n] + half_r[h, n % (tiles // 2)].astype(F32)).astype(BF16)
-            else:
-                ps[1 + h, n] = total[n].astype(BF16)
-        r_copy(h).start()
+        for n in range(half):
+            ps[1 + h, h * half + n] = (total[h * half + n] + half_r[h, n].astype(F32)).astype(BF16)
+        r_copy(h, 1).start()
 
     settle(3)
 
@@ -364,8 +397,9 @@
     def _(n):
         total[n] = partial_sum(3, n)
 
-    for h in range(2):
-        r_copy(h).wait_recv()
+    for late in range(2):
+        for h in range(2):
+            r_copy(h, late).wait_recv()
     for n in range(tiles):
         out_ref[:, n * tile:(n + 1) * tile] = (total[n] + pr[0, n].astype(F32) + pr[1, n].astype(F32)).astype(BF16)
 
@@ -395,7 +429,8 @@
             b_copy(d, i).wait_send()
     for h in range(2):
         half_copy(h).wait_send()
-        r_copy(h).wait_send()
+        for late in range(2):
+            r_copy(h, late).wait_send()
 
 
 def build(mesh, nz, ny, nx):
@@ -451,9 +486,10 @@
                 dma((nx, ny)),
                 dma((2, nz // 2, 2)),
                 dma((2, nz // 2, 2)),
-                dma((4,)),
-                dma((4,)),
                 dma((6,)),
+                dma((6,)),
+                dma((6,)),
+                pltpu.SemaphoreType.REGULAR((2, nz // 2 + 1)),
             ],
             compiler_params=pltpu.CompilerParams(
                 collective_id=0, has_side_effects=True, vmem_limit_bytes=60 * 1024 * 1024

time: 83.9 us -> 82 us (0.977)
  Pallas kernels: 82.1 us -> 80.1 us
    pallas_call x1, Pallas kernels: 82.1 us -> 80.1 us  [shards(): pl.pallas_call(functools.partial(kernel, nz, ny, nx), out_shape=jax.Shape...]
where the time goes in v3:
time: 82 us; the launch traced here: 81.8 us
  Pallas kernels  80.1 us (98%)
  local copies, waits for them, and re-layouts  1.67 us (2%)
    pallas_call x1, Pallas kernels, shards(): pl.pallas_call(functools.partial(kernel, nz, ny, nx), out_shape=jax.Shape...  80.1 us
    unnamed x1, local copies, waits for them, and re-layouts  1.67 us

profile of v3, /device:TPU:1, one launch (start us, length us, event | category | flops | bytes accessed | tf_op | source)
XLA Modules:
  0.0 81.8 jit_solution(10032895432219682057)
XLA Ops:
  0.0 80.1 %shard_map.109 = bf16[128,1024]{1,0:T(8,128)(2,1)} custom-call(bf16[512,128]{1,0:T(8,128)(2,1)} %q_ref.1, bf16[512,128]{1,0:T(8,128)(2,1)} %k_ref.1, bf16[512,128]{1,0:T(8,128)(2,1)} %v_ref.1, f32[3,3,512]{2,1,0:T(4,128)} %taps_ref.1, f32[8,8192]{1,0:T(8,128)} %h_ref.1, bf16[64,1024]{1,0:T(8,128)(2,1)} %w_ref.1, f32[144,64]{1,0:T(8,128)} %constant.10.clone.fwd_ref, ...), custom_call_target="tpu_custom_call" | custom-call | tf_op jit(solution)/shard_map/pallas_call | solution.py:448
  80.1 1.7 %copy.13 = bf16[128,1024]{1,0:T(8,128)(2,1)} copy(bf16[128,1024]{1,0:T(8,128)(2,1)} %shard_map.109) | data formatting | bytes 524288

commit v4 on v3

--- a/solution.py
+++ b/solution.py
@@ -213,6 +213,8 @@
         return result
 
     key_short = short(1)
+    for r in range(2, min(3, nz // 2 + 1)):
+        ring(r)
     word(5)
     word(6)
     value_short = short(2)
@@ -236,8 +238,6 @@
         z_copy(d).start()
 
     own_z.start()
-    for r in range(2, min(3, nz // 2 + 1)):
-        ring(r)
     for b, value in enumerate(short(0)):
         qs[b] = value
     for r in range(3, min(4, nz // 2 + 1)):
@@ -278,7 +278,7 @@
         c_copy(d).start()
 
     own_c.start()
-    for r in range(5, min(7, nz // 2 + 1)):
+    for r in range(5, min(6, nz // 2 + 1)):
         ring(r)
     own_c.wait()
 
@@ -348,19 +348,21 @@
 
     for zz in range(nz):
         rows[zz * ny * OWN:(zz + 1) * ny * OWN, :] = ar[zz].astype(F32)
+    for r in range(6, min(7, nz // 2 + 1)):
+        ring(r)
 
     gate(0)
     gate(1)
     relay(0)
+    for r in range(7, min(8, nz // 2 + 1)):
+        ring(r)
     gate(2)
     relay(1)
     gate(3)
-    for r in range(7, min(8, nz // 2 + 1)):
+    for r in range(8, min(9, nz // 2 + 1)):
         ring(r)
     settle(0)
     relay(2)
-    for r in range(8, min(9, nz // 2 + 1)):
-        ring(r)
     settle(1)
     relay(3)
     ring(nz // 2 + 1)

time: 82 us -> 80.3 us (0.979)
  Pallas kernels: 80.1 us -> 78.5 us
    pallas_call x1, Pallas kernels: 80.1 us -> 78.5 us  [shards(): pl.pallas_call(functools.partial(kernel, nz, ny, nx), out_shape=jax.Shape...]
where the time goes in v4:
time: 80.3 us; the launch traced here: 80.1 us
  Pallas kernels  78.5 us (98%)
  local copies, waits for them, and re-layouts  1.67 us (2%)
    pallas_call x1, Pallas kernels, shards(): pl.pallas_call(functools.partial(kernel, nz, ny, nx), out_shape=jax.Shape...  78.5 us
    unnamed x1, local copies, waits for them, and re-layouts  1.67 us

profile of v4, /device:TPU:1, one launch (start us, length us, event | category | flops | bytes accessed | tf_op | source)
XLA Modules:
  0.0 80.1 jit_solution(13181139765307039138)
XLA Ops:
  0.0 78.5 %shard_map.109 = bf16[128,1024]{1,0:T(8,128)(2,1)} custom-call(bf16[512,128]{1,0:T(8,128)(2,1)} %q_ref.1, bf16[512,128]{1,0:T(8,128)(2,1)} %k_ref.1, bf16[512,128]{1,0:T(8,128)(2,1)} %v_ref.1, f32[3,3,512]{2,1,0:T(4,128)} %taps_ref.1, f32[8,8192]{1,0:T(8,128)} %h_ref.1, bf16[64,1024]{1,0:T(8,128)(2,1)} %w_ref.1, f32[144,64]{1,0:T(8,128)} %constant.10.clone.fwd_ref, ...), custom_call_target="tpu_custom_call" | custom-call | tf_op jit(solution)/shard_map/pallas_call | solution.py:450
  78.5 1.7 %copy.13 = bf16[128,1024]{1,0:T(8,128)(2,1)} copy(bf16[128,1024]{1,0:T(8,128)(2,1)} %shard_map.109) | data formatting | bytes 524288

commit v5 on v4

--- a/solution.py
+++ b/solution.py
@@ -233,9 +233,9 @@
     heard()
     own_z = pltpu.make_async_copy(zs.at[z], xin.at[z], own_sem.at[4])
 
-    @pl.loop(1, nz)
-    def _(d):
-        z_copy(d).start()
+    @pl.loop(0, nz - 1)
+    def _(j):
+        z_copy(nz // 2 + jnp.where(j % 2 == 0, j // 2, -(j // 2) - 1)).start()
 
     own_z.start()
     for b, value in enumerate(short(0)):
@@ -273,9 +273,9 @@
 
     own_c = pltpu.make_async_copy(ms.at[z], ar.at[z], own_sem.at[5])
 
-    @pl.loop(1, nz)
-    def _(d):
-        c_copy(d).start()
+    @pl.loop(0, nz - 1)
+    def _(j):
+        c_copy(nz // 2 + jnp.where(j % 2 == 0, j // 2, -(j // 2) - 1)).start()
 
     own_c.start()
     for r in range(5, min(6, nz // 2 + 1)):

time: 80.3 us -> 79.3 us (0.988)
  Pallas kernels: 78.5 us -> 77.4 us
    pallas_call x1, Pallas kernels: 78.5 us -> 77.4 us  [shards(): pl.pallas_call(functools.partial(kernel, nz, ny, nx), out_shape=jax.Shape...]
where the time goes in v5:
time: 79.3 us; the launch traced here: 79.1 us
  Pallas kernels  77.4 us (98%)
  local copies, waits for them, and re-layouts  1.67 us (2%)
    pallas_call x1, Pallas kernels, shards(): pl.pallas_call(functools.partial(kernel, nz, ny, nx), out_shape=jax.Shape...  77.4 us
    unnamed x1, local copies, waits for them, and re-layouts  1.67 us

profile of v5, /device:TPU:1, one launch (start us, length us, event | category | flops | bytes accessed | tf_op | source)
XLA Modules:
  0.0 79.1 jit_solution(12902075641804101906)
XLA Ops:
  0.0 77.4 %shard_map.109 = bf16[128,1024]{1,0:T(8,128)(2,1)} custom-call(bf16[512,128]{1,0:T(8,128)(2,1)} %q_ref.1, bf16[512,128]{1,0:T(8,128)(2,1)} %k_ref.1, bf16[512,128]{1,0:T(8,128)(2,1)} %v_ref.1, f32[3,3,512]{2,1,0:T(4,128)} %taps_ref.1, f32[8,8192]{1,0:T(8,128)} %h_ref.1, bf16[64,1024]{1,0:T(8,128)(2,1)} %w_ref.1, f32[144,64]{1,0:T(8,128)} %constant.10.clone.fwd_ref, ...), custom_call_target="tpu_custom_call" | custom-call | tf_op jit(solution)/shard_map/pallas_call | solution.py:450
  77.5 1.7 %copy.13 = bf16[128,1024]{1,0:T(8,128)(2,1)} copy(bf16[128,1024]{1,0:T(8,128)(2,1)} %shard_map.109) | data formatting | bytes 524288

commit v6 on v5

--- a/solution.py
+++ b/solution.py
@@ -353,14 +353,14 @@
 
     gate(0)
     gate(1)
+    for r in range(7, min(8, nz // 2 + 1)):
+        ring(r)
     relay(0)
-    for r in range(7, min(8, nz // 2 + 1)):
-        ring(r)
     gate(2)
     relay(1)
+    for r in range(8, min(9, nz // 2 + 1)):
+        ring(r)
     gate(3)
-    for r in range(8, min(9, nz // 2 + 1)):
-        ring(r)
     settle(0)
     relay(2)
     settle(1)

time: 79.3 us -> 79.3 us (level)
  no operation moved by 1% of the time
where the time goes in v6:
time: 79.3 us; the launch traced here: 79.1 us
  Pallas kernels  77.4 us (98%)
  local copies, waits for them, and re-layouts  1.67 us (2%)
    pallas_call x1, Pallas kernels, shards(): pl.pallas_call(functools.partial(kernel, nz, ny, nx), out_shape=jax.Shape...  77.4 us
    unnamed x1, local copies, waits for them, and re-layouts  1.67 us

profile of v6, /device:TPU:1, one launch (start us, length us, event | category | flops | bytes accessed | tf_op | source)
XLA Modules:
  0.0 79.1 jit_solution(12799659169764483025)
XLA Ops:
  0.0 77.4 %shard_map.109 = bf16[128,1024]{1,0:T(8,128)(2,1)} custom-call(bf16[512,128]{1,0:T(8,128)(2,1)} %q_ref.1, bf16[512,128]{1,0:T(8,128)(2,1)} %k_ref.1, bf16[512,128]{1,0:T(8,128)(2,1)} %v_ref.1, f32[3,3,512]{2,1,0:T(4,128)} %taps_ref.1, f32[8,8192]{1,0:T(8,128)} %h_ref.1, bf16[64,1024]{1,0:T(8,128)(2,1)} %w_ref.1, f32[144,64]{1,0:T(8,128)} %constant.10.clone.fwd_ref, ...), custom_call_target="tpu_custom_call" | custom-call | tf_op jit(solution)/shard_map/pallas_call | solution.py:450
  77.4 1.7 %copy.13 = bf16[128,1024]{1,0:T(8,128)(2,1)} copy(bf16[128,1024]{1,0:T(8,128)(2,1)} %shard_map.109) | data formatting | bytes 524288
